TPU v7x, 128 devices: a whole 4x4x4 slice. The times are simulated.
128 devices in a mesh: pr: 16 (over z, x), pc: 8 (over y, core).
Axes of the slice: x: 4, y: 4, z: 4, core: 2. Of those that a mesh axis runs over, the one named last changes fastest.
Arguments:
- trailing: float32 [20480, 20480], P('pr', 'pc'), may hold values from -25 to 25, as said below
- v_panels: float32 [6, 32, 20480], P(None, None, ('pr', 'pc')), may hold values from -0.078125 to 0.078125
- t_panels: float32 [6, 32, 32], replicated, may hold values from -0.2 to 0.5, as said below
Outputs:
- updated: float32 [20480, 20480], P('pr', 'pc')
- w_panels: float32 [6, 32, 20480], P(None, None, ('pr', 'pc'))
Inputs may be any that keep to these rules, and one draw needn't show every extreme that they name: trailing is exactly symmetric. `t_panels`: each panel's factor is upper triangular with diagonal entries of 0.25 to 0.5.
All inputs are finite; a program needn't handle non-finite values.
Results may differ from a plain program's by a relative error of at most 0.00013.
Values sent between devices are 32-bit elements; how exact they have to be, the bound alone decides.
A program may use at most 128 MiB of HBM per device.

v0:
```python
import jax
import jax.numpy as jnp
from jax import lax
from jax.sharding import PartitionSpec as P


def broadcast(value, axis, source):
    kept = jnp.where(lax.axis_index(axis) == source, value, 0).astype(value.dtype)
    return lax.psum(kept, axis)


def contract(left_side, right_side, left_dim, right_dim):
    return lax.dot_general(
        left_side,
        right_side,
        (((left_dim,), (right_dim,)), ((), ())),
        precision=lax.Precision.HIGHEST,
        preferred_element_type=jnp.float32,
    )


def fetch_v_columns(v_row, col_rank, ratio):
    pieces = []
    for offset in range(ratio):
        pieces.append(broadcast(v_row, "pr", col_rank * ratio + offset))
    return jnp.concatenate(pieces, axis=1)


def fetch_w_columns(w_row, col_rank, ratio):
    pieces = []
    for offset in range(ratio):
        pieces.append(broadcast(w_row, "pr", col_rank * ratio + offset))
    return jnp.concatenate(pieces, axis=1)


def per_device(trailing, v_panels, t_panels):
    matrix = trailing
    rows_here = matrix.shape[0]
    col_rank = lax.axis_index("pc")
    ratio = lax.axis_size("pr") // lax.axis_size("pc")
    share = rows_here // lax.axis_size("pc")
    w_blocks = []
    for panel in range(v_panels.shape[0]):
        v_row = lax.all_gather(v_panels[panel], "pc", axis=1, tiled=True)
        v_col = fetch_v_columns(v_row, col_rank, ratio)
        factor = t_panels[panel]
        partial_value = contract(v_col, matrix, 1, 1)
        x_row = lax.psum(partial_value, "pc")
        gram_block = lax.psum(contract(v_row, x_row, 1, 1), "pr")
        middle = contract(contract(factor, gram_block, 0, 0), factor, 1, 0)
        w_row = contract(factor, x_row, 0, 0) - 0.5 * contract(middle, v_row, 0, 0)
        w_col = fetch_w_columns(w_row, col_rank, ratio)
        left_side = jnp.concatenate([v_row, w_row], axis=0)
        right_side = jnp.concatenate([w_col, v_col], axis=0)
        matrix = matrix - contract(left_side, right_side, 0, 0)
        w_blocks.append(lax.dynamic_slice_in_dim(w_row, col_rank * share, share, 1))
    return (matrix, jnp.stack(w_blocks))


def solution(mesh):
    return jax.shard_map(
        per_device,
        mesh=mesh,
        in_specs=(P("pr", "pc"), P(None, None, ("pr", "pc")), P()),
        out_specs=(P("pr", "pc"), P(None, None, ("pr", "pc"))),
        check_vma=False,
    )
```

profile of v0, /device:TPU:0, one launch (start us, length us, event | category | flops | bytes accessed | tf_op | source)
XLA Modules:
  0.0 1610.5 jit_solution(2257900202977496059)
XLA Ops:
  36.9 71.9 %all-reduce.45.cloned.1.call-done = (f32[32,1280]{1,0:T(8,128)}, f32[32,1280]{1,0:T(8,128)}) async-done(((f32[32,1280]{1,0:T(8,128)}, f32[32,1280]{1,0:T(8,128)}), (f32[32,1280]{1,0:T(8,128)}, f32[32,1280]{1,0:T(8,128)})) %all-reduce.45.cloned.1.call-update) | async-done | bytes 327696 | tf_op jit(solution)/shard_map/psum | solution.py:9
  110.6 15.3 fusion.109
  126.8 56.5 %all-reduce.21.cloned.1.call-done = f32[32,1280]{1,0:T(8,128)} async-done(((f32[32,1280]{1,0:T(8,128)}), f32[32,1280]{1,0:T(8,128)}) %all-reduce.21.cloned.1.call-update) | async-done | bytes 163856 | tf_op jit(solution)/shard_map/psum | solution.py:48
  184.6 74.6 %psum.255 = f32[32,32]{0,1:T(8,128)S(1)} all-reduce(f32[32,32]{0,1:T(8,128)S(1)} %convolution_bitcast_fusion.11), channel_id=1, replica_groups=mesh['pr'=16,'pc'=8] {'pr'}, use_global_device_ids=true, to_apply=%region_3.4 | all-reduce | flops 1024 | bytes 8192 | tf_op jit(solution)/shard_map/psum | solution.py:49
  276.3 65.5 %all-reduce.43.cloned.1.call-done = (f32[32,1280]{1,0:T(8,128)}, f32[32,1280]{1,0:T(8,128)}, f32[32,1280]{1,0:T(8,128)}, f32[32,1280]{1,0:T(8,128)}) async-done(((f32[32,1280]{1,0:T(8,128)}, f32[32,1280]{1,0:T(8,128)}, f32[32,1280]{1,0:T(8,128)}, f32[32,1280]{1,0:T(8,128)}), (f32[32,1280]{1,0:T(8,128)}, f32[32,1280]{1,0:T(8,128)}, f32[32,1280]{1,0:T(8,128)}, ...) | async-done | bytes 655376 | tf_op jit(solution)/shard_map/psum | solution.py:9
  343.7 14.6 convolution_subtract_fusion.5
  376.5 56.5 %all-reduce.23.cloned.1.call-done = f32[32,1280]{1,0:T(8,128)} async-done(((f32[32,1280]{1,0:T(8,128)}), f32[32,1280]{1,0:T(8,128)}) %all-reduce.23.cloned.1.call-update) | async-done | bytes 163856 | tf_op jit(solution)/shard_map/psum | solution.py:48
  434.4 74.6 %psum.261 = f32[32,32]{0,1:T(8,128)S(1)} all-reduce(f32[32,32]{0,1:T(8,128)S(1)} %convolution_bitcast_fusion.10), channel_id=1, replica_groups=mesh['pr'=16,'pc'=8] {'pr'}, use_global_device_ids=true, to_apply=%region_9.10 | all-reduce | flops 1024 | bytes 8192 | tf_op jit(solution)/shard_map/psum | solution.py:49
  537.6 54.1 %all-reduce.41.cloned.1.call-done = (f32[32,1280]{1,0:T(8,128)}, f32[32,1280]{1,0:T(8,128)}, f32[32,1280]{1,0:T(8,128)}, f32[32,1280]{1,0:T(8,128)}) async-done(((f32[32,1280]{1,0:T(8,128)}, f32[32,1280]{1,0:T(8,128)}, f32[32,1280]{1,0:T(8,128)}, f32[32,1280]{1,0:T(8,128)}), (f32[32,1280]{1,0:T(8,128)}, f32[32,1280]{1,0:T(8,128)}, f32[32,1280]{1,0:T(8,128)}, ...) | async-done | bytes 655376 | tf_op jit(solution)/shard_map/psum | solution.py:9
  626.0 56.5 %all-reduce.25.cloned.1.call-done = f32[32,1280]{1,0:T(8,128)} async-done(((f32[32,1280]{1,0:T(8,128)}), f32[32,1280]{1,0:T(8,128)}) %all-reduce.25.cloned.1.call-update) | async-done | bytes 163856 | tf_op jit(solution)/shard_map/psum | solution.py:48
  683.9 74.6 %psum.267 = f32[32,32]{0,1:T(8,128)S(1)} all-reduce(f32[32,32]{0,1:T(8,128)S(1)} %convolution_bitcast_fusion.9), channel_id=1, replica_groups=mesh['pr'=16,'pc'=8] {'pr'}, use_global_device_ids=true, to_apply=%region_15.16 | all-reduce | flops 1024 | bytes 8192 | tf_op jit(solution)/shard_map/psum | solution.py:49
  775.7 65.4 %all-reduce.39.cloned.1.call-done = (f32[32,1280]{1,0:T(8,128)}, f32[32,1280]{1,0:T(8,128)}, f32[32,1280]{1,0:T(8,128)}, f32[32,1280]{1,0:T(8,128)}) async-done(((f32[32,1280]{1,0:T(8,128)}, f32[32,1280]{1,0:T(8,128)}, f32[32,1280]{1,0:T(8,128)}, f32[32,1280]{1,0:T(8,128)}), (f32[32,1280]{1,0:T(8,128)}, f32[32,1280]{1,0:T(8,128)}, f32[32,1280]{1,0:T(8,128)}, ...) | async-done | bytes 655376 | tf_op jit(solution)/shard_map/psum | solution.py:9
  843.0 14.2 convolution_subtract_fusion.3
  875.5 56.5 %all-reduce.27.cloned.1.call-done = f32[32,1280]{1,0:T(8,128)} async-done(((f32[32,1280]{1,0:T(8,128)}), f32[32,1280]{1,0:T(8,128)}) %all-reduce.27.cloned.1.call-update) | async-done | bytes 163856 | tf_op jit(solution)/shard_map/psum | solution.py:48
  933.4 74.6 %psum.273 = f32[32,32]{0,1:T(8,128)S(1)} all-reduce(f32[32,32]{0,1:T(8,128)S(1)} %convolution_bitcast_fusion.8), channel_id=1, replica_groups=mesh['pr'=16,'pc'=8] {'pr'}, use_global_device_ids=true, to_apply=%region_21.22 | all-reduce | flops 1024 | bytes 8192 | tf_op jit(solution)/shard_map/psum | solution.py:49
  1025.0 65.7 %all-reduce.37.cloned.1.call-done = (f32[32,1280]{1,0:T(8,128)}, f32[32,1280]{1,0:T(8,128)}, f32[32,1280]{1,0:T(8,128)}, f32[32,1280]{1,0:T(8,128)}) async-done(((f32[32,1280]{1,0:T(8,128)}, f32[32,1280]{1,0:T(8,128)}, f32[32,1280]{1,0:T(8,128)}, f32[32,1280]{1,0:T(8,128)}), (f32[32,1280]{1,0:T(8,128)}, f32[32,1280]{1,0:T(8,128)}, f32[32,1280]{1,0:T(8,128)}, ...) | async-done | bytes 655376 | tf_op jit(solution)/shard_map/psum | solution.py:9
  1125.0 56.5 %all-reduce.29.cloned.1.call-done = f32[32,1280]{1,0:T(8,128)} async-done(((f32[32,1280]{1,0:T(8,128)}), f32[32,1280]{1,0:T(8,128)}) %all-reduce.29.cloned.1.call-update) | async-done | bytes 163856 | tf_op jit(solution)/shard_map/psum | solution.py:48
  1182.9 74.6 %psum.279 = f32[32,32]{0,1:T(8,128)S(1)} all-reduce(f32[32,32]{0,1:T(8,128)S(1)} %convolution_bitcast_fusion.7), channel_id=1, replica_groups=mesh['pr'=16,'pc'=8] {'pr'}, use_global_device_ids=true, to_apply=%region_27.28 | all-reduce | flops 1024 | bytes 8192 | tf_op jit(solution)/shard_map/psum | solution.py:49
  1260.8 79.3 %all-reduce.35.cloned.1.call-done = (f32[32,1280]{1,0:T(8,128)}, f32[32,1280]{1,0:T(8,128)}, f32[32,1280]{1,0:T(8,128)}, f32[32,1280]{1,0:T(8,128)}) async-done(((f32[32,1280]{1,0:T(8,128)}, f32[32,1280]{1,0:T(8,128)}, f32[32,1280]{1,0:T(8,128)}, f32[32,1280]{1,0:T(8,128)}), (f32[32,1280]{1,0:T(8,128)}, f32[32,1280]{1,0:T(8,128)}, f32[32,1280]{1,0:T(8,128)}, ...) | async-done | bytes 655376 | tf_op jit(solution)/shard_map/psum | solution.py:9
  1342.0 14.4 convolution_subtract_fusion.1
  1374.0 57.2 %all-reduce.31.cloned.1.call-done = f32[32,1280]{1,0:T(8,128)} async-done(((f32[32,1280]{1,0:T(8,128)}), f32[32,1280]{1,0:T(8,128)}) %all-reduce.31.cloned.1.call-update) | async-done | bytes 163856 | tf_op jit(solution)/shard_map/psum | solution.py:48
  1432.5 74.9 %psum.285 = f32[32,32]{0,1:T(8,128)S(1)} all-reduce(f32[32,32]{0,1:T(8,128)S(1)} %convolution_bitcast_fusion.6), channel_id=1, replica_groups=mesh['pr'=16,'pc'=8] {'pr'}, use_global_device_ids=true, to_apply=%region_33.34 | all-reduce | flops 1024 | bytes 8192 | tf_op jit(solution)/shard_map/psum | solution.py:49
  1510.9 77.3 %all-reduce.33.cloned.1.call-done = (f32[32,1280]{1,0:T(8,128)}, f32[32,1280]{1,0:T(8,128)}) async-done(((f32[32,1280]{1,0:T(8,128)}, f32[32,1280]{1,0:T(8,128)}), (f32[32,1280]{1,0:T(8,128)}, f32[32,1280]{1,0:T(8,128)})) %all-reduce.33.cloned.1.call-update) | async-done | bytes 327696 | tf_op jit(solution)/shard_map/psum | solution.py:9
  1588.1 15.4 convolution_subtract_fusion
  (120 shorter events, 255.3 us)
Async XLA Ops:
  7.2 252.0 %copy-start.5 = (f32[6,32,32]{2,1,0:T(8,128)S(1)}, f32[6,32,32]{2,1,0:T(8,128)}, u32[]{:S(2)}) copy-start(f32[6,32,32]{2,1,0:T(8,128)} %param.5) | copy-start | bytes 73732
  7.2 101.6 %all-reduce.45.cloned.1.call-start = ((), (), s32[]{:S(2)}) async-start(), calls=%async_computation.12 | async-start | bytes 655360 | tf_op jit(solution)/shard_map/psum | solution.py:9
  23.2 160.1 %all-reduce.21.cloned.1.call-start = ((), (), s32[]{:S(2)}) async-start(), calls=%async_computation | async-start | bytes 327680 | tf_op jit(solution)/shard_map/psum | solution.py:48
  126.0 215.9 %all-reduce.43.cloned.1.call-start = ((), (), s32[]{:S(2)}) async-start(), calls=%async_computation.11 | async-start | bytes 1310720 | tf_op jit(solution)/shard_map/psum | solution.py:9
  262.4 170.6 %all-reduce.23.cloned.1.call-start = ((), (), s32[]{:S(2)}) async-start(), calls=%async_computation.1 | async-start | bytes 327680 | tf_op jit(solution)/shard_map/psum | solution.py:48
  358.3 5.0 copy-start.3
  375.7 216.0 %all-reduce.41.cloned.1.call-start = ((), (), s32[]{:S(2)}) async-start(), calls=%async_computation.10 | async-start | bytes 1310720 | tf_op jit(solution)/shard_map/psum | solution.py:9
  512.1 170.4 %all-reduce.25.cloned.1.call-start = ((), (), s32[]{:S(2)}) async-start(), calls=%async_computation.2 | async-start | bytes 327680 | tf_op jit(solution)/shard_map/psum | solution.py:48
  607.8 5.0 copy-start.2
  625.2 215.9 %all-reduce.39.cloned.1.call-start = ((), (), s32[]{:S(2)}) async-start(), calls=%async_computation.9 | async-start | bytes 1310720 | tf_op jit(solution)/shard_map/psum | solution.py:9
  761.6 170.4 %all-reduce.27.cloned.1.call-start = ((), (), s32[]{:S(2)}) async-start(), calls=%async_computation.3 | async-start | bytes 327680 | tf_op jit(solution)/shard_map/psum | solution.py:48
  857.3 5.0 copy-start.1
  874.7 216.0 %all-reduce.37.cloned.1.call-start = ((), (), s32[]{:S(2)}) async-start(), calls=%async_computation.8 | async-start | bytes 1310720 | tf_op jit(solution)/shard_map/psum | solution.py:9
  1011.1 170.4 %all-reduce.29.cloned.1.call-start = ((), (), s32[]{:S(2)}) async-start(), calls=%async_computation.4 | async-start | bytes 327680 | tf_op jit(solution)/shard_map/psum | solution.py:48
  1106.8 5.0 copy-start
  1124.2 215.9 %all-reduce.35.cloned.1.call-start = ((), (), s32[]{:S(2)}) async-start(), calls=%async_computation.7 | async-start | bytes 1310720 | tf_op jit(solution)/shard_map/psum | solution.py:9
  1260.6 170.6 %all-reduce.31.cloned.1.call-start = ((), (), s32[]{:S(2)}) async-start(), calls=%async_computation.5 | async-start | bytes 327680 | tf_op jit(solution)/shard_map/psum | solution.py:48
  1356.5 5.0 copy-start.4
  1373.9 214.3 %all-reduce.33.cloned.1.call-start = ((), (), s32[]{:S(2)}) async-start(), calls=%async_computation.6 | async-start | bytes 655360 | tf_op jit(solution)/shard_map/psum | solution.py:9
  1510.9 92.7 %copy-start.6 = (f32[6,32,160]{2,1,0:T(8,128)}, f32[6,32,160]{2,1,0:T(8,128)S(1)}, u32[]{:S(2)}) copy-start(f32[6,32,160]{2,1,0:T(8,128)S(1)} %constant_dynamic-update-slice_fusion.12) | copy-start | bytes 368644
Sparse Core Ops, SparseCore 0:
  23.3 85.4 all-reduce.44
  126.1 57.1 all-reduce.20
  262.5 79.3 all-reduce.42
  375.8 57.1 all-reduce.22
  512.2 79.4 all-reduce.40
  625.3 57.1 all-reduce.24
  761.7 79.3 all-reduce.38
  874.8 57.1 all-reduce.26
  1011.2 79.4 all-reduce.36
  1124.3 57.1 all-reduce.28
  1260.7 79.3 all-reduce.34
  1374.0 57.1 all-reduce.30
  1510.7 77.3 all-reduce.32
where the time goes:
time: 1620 us; the launch traced here: 1610 us
  waiting for transfers between devices  819 us (51%)
  blocking collectives  528 us (33%)
  matrix products  192 us (12%)
  local copies, waits for them, and re-layouts  52.1 us (3%)
    psum x7, waiting for transfers between devices, broadcast(): return lax.psum(kept, axis)  479 us
    psum x6, blocking collectives, per_device(): gram_block = lax.psum(contract(v_row, x_row, 1, 1), 'pr')  448 us
    psum x6, waiting for transfers between devices, per_device(): x_row = lax.psum(partial_value, 'pc')  340 us
    dot_general x42, matrix products, contract(): lax.dot_general(left_side, right_side, (((left_dim,), (right_dim,)), ((),...  192 us
    all_gather x6, blocking collectives, per_device(): v_row = lax.all_gather(v_panels[panel], 'pc', axis=1, tiled=True)  80.3 us
  transfers between devices with their start and end apart: 13, of which 13 were waited for; matrix products, arithmetic and copies ran while one was open for 1% of the time, Pallas kernels for 0%

commit v1 on v0

--- a/solution.py
+++ b/solution.py
@@ -41,7 +41,14 @@
     share = rows_here // lax.axis_size("pc")
     w_blocks = []
     for panel in range(v_panels.shape[0]):
-        v_row = lax.all_gather(v_panels[panel], "pc", axis=1, tiled=True)
+        ring = [v_panels[panel]]
+        for hop in range(7):
+            ring.append(lax.ppermute(ring[-1], "pc", [(dev, (dev + 1) % 8) for dev in range(8)]))
+        v_row = jnp.roll(
+            jnp.concatenate(ring[::-1], axis=1),
+            (lax.axis_index("pc") + 1) * ring[0].shape[1],
+            axis=1,
+        )
         v_col = fetch_v_columns(v_row, col_rank, ratio)
         factor = t_panels[panel]
         partial_value = contract(v_col, matrix, 1, 1)

time: 1620 us -> 1640 us (1.012)
  waiting for transfers between devices: 819 us -> 925 us
  blocking collectives: 528 us -> 448 us
    ppermute x0 -> x42, waiting for transfers between devices: none -> 177 us  [per_device(): lax.ppermute(ring[-1], 'pc', [(dev, (dev + 1) % 8) for dev in range(8)])]
    all_gather x6 -> x0, blocking collectives: 80.3 us -> none  [per_device(): v_row = lax.all_gather(v_panels[panel], 'pc', axis=1, tiled=True)]
    psum x7, waiting for transfers between devices: 479 us -> 407 us  [broadcast(): return lax.psum(kept, axis)]
  transfers between devices with their start and end apart: 13 -> 55, of which waited for: 13 -> 54; matrix products, arithmetic and copies ran while one was open for 1% -> 1% of each run, Pallas kernels for 0% -> 0%
where the time goes in v1:
time: 1640 us
  waiting for transfers between devices  925 us (56%)
  blocking collectives  448 us (27%)
  matrix products  201 us (12%)
  local copies, waits for them, and re-layouts  38 us (2%)
    psum x6, blocking collectives, per_device(): gram_block = lax.psum(contract(v_row, x_row, 1, 1), 'pr')  448 us
    psum x7, waiting for transfers between devices, broadcast(): return lax.psum(kept, axis)  407 us
    psum x6, waiting for transfers between devices, per_device(): x_row = lax.psum(partial_value, 'pc')  340 us
    dot_general x42, matrix products, contract(): lax.dot_general(left_side, right_side, (((left_dim,), (right_dim,)), ((),...  201 us
    ppermute x42, waiting for transfers between devices, per_device(): lax.ppermute(ring[-1], 'pc', [(dev, (dev + 1) % 8) for dev in range(8)])  177 us
  transfers between devices with their start and end apart: 55, of which 54 were waited for; matrix products, arithmetic and copies ran while one was open for 1% of the time, Pallas kernels for 0%

profile of v1, /device:TPU:0, one launch (start us, length us, event | category | flops | bytes accessed | tf_op | source)
XLA Modules:
  0.0 1635.8 jit_solution(17727349386555279008)
XLA Ops:
  60.9 64.4 %all-reduce.45.cloned.1.call-done = (f32[32,1280]{1,0:T(8,128)}, f32[32,1280]{1,0:T(8,128)}) async-done(((f32[32,1280]{1,0:T(8,128)}, f32[32,1280]{1,0:T(8,128)}), (f32[32,1280]{1,0:T(8,128)}, f32[32,1280]{1,0:T(8,128)})) %all-reduce.45.cloned.1.call-update) | async-done | bytes 327696 | tf_op jit(solution)/shard_map/psum | solution.py:9
  127.2 15.3 fusion.120
  143.3 56.5 %all-reduce.21.cloned.1.call-done = f32[32,1280]{1,0:T(8,128)} async-done(((f32[32,1280]{1,0:T(8,128)}), f32[32,1280]{1,0:T(8,128)}) %all-reduce.21.cloned.1.call-update) | async-done | bytes 163856 | tf_op jit(solution)/shard_map/psum | solution.py:55
  201.0 74.6 %psum.255 = f32[32,32]{1,0:T(8,128)S(1)} all-reduce(f32[32,32]{1,0:T(8,128)S(1)} %fusion.121), channel_id=1, replica_groups=mesh['pr'=16,'pc'=8] {'pr'}, use_global_device_ids=true, to_apply=%region_3.5 | all-reduce | flops 1024 | bytes 8192 | tf_op jit(solution)/shard_map/psum | solution.py:56
  311.4 46.4 %all-reduce.43.cloned.1.call-done = (f32[32,1280]{1,0:T(8,128)}, f32[32,1280]{1,0:T(8,128)}, f32[32,1280]{1,0:T(8,128)}, f32[32,1280]{1,0:T(8,128)}) async-done(((f32[32,1280]{1,0:T(8,128)}, f32[32,1280]{1,0:T(8,128)}, f32[32,1280]{1,0:T(8,128)}, f32[32,1280]{1,0:T(8,128)}), (f32[32,1280]{1,0:T(8,128)}, f32[32,1280]{1,0:T(8,128)}, f32[32,1280]{1,0:T(8,128)}, ...) | async-done | bytes 655376 | tf_op jit(solution)/shard_map/psum | solution.py:9
  359.7 14.6 convolution_subtract_fusion.5
  392.4 56.6 %all-reduce.23.cloned.1.call-done = f32[32,1280]{1,0:T(8,128)} async-done(((f32[32,1280]{1,0:T(8,128)}), f32[32,1280]{1,0:T(8,128)}) %all-reduce.23.cloned.1.call-update) | async-done | bytes 163856 | tf_op jit(solution)/shard_map/psum | solution.py:55
  450.2 74.6 %psum.261 = f32[32,32]{1,0:T(8,128)S(1)} all-reduce(f32[32,32]{1,0:T(8,128)S(1)} %fusion.123), channel_id=1, replica_groups=mesh['pr'=16,'pc'=8] {'pr'}, use_global_device_ids=true, to_apply=%region_9.11 | all-reduce | flops 1024 | bytes 8192 | tf_op jit(solution)/shard_map/psum | solution.py:56
  560.4 46.6 %all-reduce.41.cloned.1.call-done = (f32[32,1280]{1,0:T(8,128)}, f32[32,1280]{1,0:T(8,128)}, f32[32,1280]{1,0:T(8,128)}, f32[32,1280]{1,0:T(8,128)}) async-done(((f32[32,1280]{1,0:T(8,128)}, f32[32,1280]{1,0:T(8,128)}, f32[32,1280]{1,0:T(8,128)}, f32[32,1280]{1,0:T(8,128)}), (f32[32,1280]{1,0:T(8,128)}, f32[32,1280]{1,0:T(8,128)}, f32[32,1280]{1,0:T(8,128)}, ...) | async-done | bytes 655376 | tf_op jit(solution)/shard_map/psum | solution.py:9
  608.9 25.8 %convolution_subtract_fusion.4 = f32[1280,2560]{1,0:T(8,128)S(1)} fusion(f32[1280,2560]{1,0:T(8,128)} %copy-done.2, f32[32,2560]{1,0:T(8,128)S(1)} %constant_dynamic-update-slice_fusion.2, f32[32,1280]{1,0:T(8,128)} %get-tuple-element.17, f32[32,1280]{1,0:T(8,128)} %get-tuple-element.18, f32[32,1280]{1,0:T(8,128)S(1)} %get-tuple-element.58, ...), kind=kOutput, calls=%fused_computation.4 | convolution fusion | flops 2520268800 | bytes 27197440 | tf_op jit(solution)/shard_map/dot_general | solution.py:13
  652.8 56.6 %all-reduce.25.cloned.1.call-done = f32[32,1280]{1,0:T(8,128)} async-done(((f32[32,1280]{1,0:T(8,128)}), f32[32,1280]{1,0:T(8,128)}) %all-reduce.25.cloned.1.call-update) | async-done | bytes 163856 | tf_op jit(solution)/shard_map/psum | solution.py:55
  710.6 74.6 %psum.267 = f32[32,32]{1,0:T(8,128)S(1)} all-reduce(f32[32,32]{1,0:T(8,128)S(1)} %fusion.125), channel_id=1, replica_groups=mesh['pr'=16,'pc'=8] {'pr'}, use_global_device_ids=true, to_apply=%region_15.17 | all-reduce | flops 1024 | bytes 8192 | tf_op jit(solution)/shard_map/psum | solution.py:56
  820.8 46.7 %all-reduce.39.cloned.1.call-done = (f32[32,1280]{1,0:T(8,128)}, f32[32,1280]{1,0:T(8,128)}, f32[32,1280]{1,0:T(8,128)}, f32[32,1280]{1,0:T(8,128)}) async-done(((f32[32,1280]{1,0:T(8,128)}, f32[32,1280]{1,0:T(8,128)}, f32[32,1280]{1,0:T(8,128)}, f32[32,1280]{1,0:T(8,128)}), (f32[32,1280]{1,0:T(8,128)}, f32[32,1280]{1,0:T(8,128)}, f32[32,1280]{1,0:T(8,128)}, ...) | async-done | bytes 655376 | tf_op jit(solution)/shard_map/psum | solution.py:9
  869.4 14.7 convolution_subtract_fusion.3
  902.2 56.6 %all-reduce.27.cloned.1.call-done = f32[32,1280]{1,0:T(8,128)} async-done(((f32[32,1280]{1,0:T(8,128)}), f32[32,1280]{1,0:T(8,128)}) %all-reduce.27.cloned.1.call-update) | async-done | bytes 163856 | tf_op jit(solution)/shard_map/psum | solution.py:55
  959.9 74.6 %psum.273 = f32[32,32]{1,0:T(8,128)S(1)} all-reduce(f32[32,32]{1,0:T(8,128)S(1)} %fusion.127), channel_id=1, replica_groups=mesh['pr'=16,'pc'=8] {'pr'}, use_global_device_ids=true, to_apply=%region_21.23 | all-reduce | flops 1024 | bytes 8192 | tf_op jit(solution)/shard_map/psum | solution.py:56
  1070.2 46.6 %all-reduce.37.cloned.1.call-done = (f32[32,1280]{1,0:T(8,128)}, f32[32,1280]{1,0:T(8,128)}, f32[32,1280]{1,0:T(8,128)}, f32[32,1280]{1,0:T(8,128)}) async-done(((f32[32,1280]{1,0:T(8,128)}, f32[32,1280]{1,0:T(8,128)}, f32[32,1280]{1,0:T(8,128)}, f32[32,1280]{1,0:T(8,128)}), (f32[32,1280]{1,0:T(8,128)}, f32[32,1280]{1,0:T(8,128)}, f32[32,1280]{1,0:T(8,128)}, ...) | async-done | bytes 655376 | tf_op jit(solution)/shard_map/psum | solution.py:9
  1151.2 56.6 %all-reduce.29.cloned.1.call-done = f32[32,1280]{1,0:T(8,128)} async-done(((f32[32,1280]{1,0:T(8,128)}), f32[32,1280]{1,0:T(8,128)}) %all-reduce.29.cloned.1.call-update) | async-done | bytes 163856 | tf_op jit(solution)/shard_map/psum | solution.py:55
  1209.0 74.6 %psum.279 = f32[32,32]{1,0:T(8,128)S(1)} all-reduce(f32[32,32]{1,0:T(8,128)S(1)} %fusion.129), channel_id=1, replica_groups=mesh['pr'=16,'pc'=8] {'pr'}, use_global_device_ids=true, to_apply=%region_27.29 | all-reduce | flops 1024 | bytes 8192 | tf_op jit(solution)/shard_map/psum | solution.py:56
  1286.6 79.4 %all-reduce.35.cloned.1.call-done = (f32[32,1280]{1,0:T(8,128)}, f32[32,1280]{1,0:T(8,128)}, f32[32,1280]{1,0:T(8,128)}, f32[32,1280]{1,0:T(8,128)}) async-done(((f32[32,1280]{1,0:T(8,128)}, f32[32,1280]{1,0:T(8,128)}, f32[32,1280]{1,0:T(8,128)}, f32[32,1280]{1,0:T(8,128)}), (f32[32,1280]{1,0:T(8,128)}, f32[32,1280]{1,0:T(8,128)}, f32[32,1280]{1,0:T(8,128)}, ...) | async-done | bytes 655376 | tf_op jit(solution)/shard_map/psum | solution.py:9
  1399.8 57.2 %all-reduce.31.cloned.1.call-done = f32[32,1280]{1,0:T(8,128)} async-done(((f32[32,1280]{1,0:T(8,128)}), f32[32,1280]{1,0:T(8,128)}) %all-reduce.31.cloned.1.call-update) | async-done | bytes 163856 | tf_op jit(solution)/shard_map/psum | solution.py:55
  1458.2 74.9 %psum.285 = f32[32,32]{1,0:T(8,128)S(1)} all-reduce(f32[32,32]{1,0:T(8,128)S(1)} %fusion.131), channel_id=1, replica_groups=mesh['pr'=16,'pc'=8] {'pr'}, use_global_device_ids=true, to_apply=%region_33.35 | all-reduce | flops 1024 | bytes 8192 | tf_op jit(solution)/shard_map/psum | solution.py:56
  1536.1 77.3 %all-reduce.33.cloned.1.call-done = (f32[32,1280]{1,0:T(8,128)}, f32[32,1280]{1,0:T(8,128)}) async-done(((f32[32,1280]{1,0:T(8,128)}, f32[32,1280]{1,0:T(8,128)}), (f32[32,1280]{1,0:T(8,128)}, f32[32,1280]{1,0:T(8,128)})) %all-reduce.33.cloned.1.call-update) | async-done | bytes 327696 | tf_op jit(solution)/shard_map/psum | solution.py:9
  1613.4 15.4 convolution_subtract_fusion
  (198 shorter events, 340.3 us)
Async XLA Ops:
  7.2 118.1 %all-reduce.45.cloned.1.call-start = ((), (), s32[]{:S(2)}) async-start(), calls=%async_computation.12 | async-start | bytes 655360 | tf_op jit(solution)/shard_map/psum | solution.py:9
  8.1 4.6 collective-permute-start
  26.3 4.9 collective-permute-start.7
  30.8 4.6 collective-permute-start.5
  35.7 5.9 collective-permute-start.9
  41.6 158.1 %all-reduce.21.cloned.1.call-start = ((), (), s32[]{:S(2)}) async-start(), calls=%async_computation | async-start | bytes 327680 | tf_op jit(solution)/shard_map/psum | solution.py:55
  41.7 4.6 collective-permute-start.10
  50.8 4.6 collective-permute-start.12
  142.5 215.3 %all-reduce.43.cloned.1.call-start = ((), (), s32[]{:S(2)}) async-start(), calls=%async_computation.11 | async-start | bytes 1310720 | tf_op jit(solution)/shard_map/psum | solution.py:9
  278.3 170.7 %all-reduce.23.cloned.1.call-start = ((), (), s32[]{:S(2)}) async-start(), calls=%async_computation.1 | async-start | bytes 327680 | tf_op jit(solution)/shard_map/psum | solution.py:55
  278.6 4.6 collective-permute-start.14
  292.2 4.6 collective-permute-start.17
  391.7 215.3 %all-reduce.41.cloned.1.call-start = ((), (), s32[]{:S(2)}) async-start(), calls=%async_computation.10 | async-start | bytes 1310720 | tf_op jit(solution)/shard_map/psum | solution.py:9
  527.5 181.9 %all-reduce.25.cloned.1.call-start = ((), (), s32[]{:S(2)}) async-start(), calls=%async_computation.2 | async-start | bytes 327680 | tf_op jit(solution)/shard_map/psum | solution.py:55
  527.6 4.6 collective-permute-start.21
  652.1 215.4 %all-reduce.39.cloned.1.call-start = ((), (), s32[]{:S(2)}) async-start(), calls=%async_computation.9 | async-start | bytes 1310720 | tf_op jit(solution)/shard_map/psum | solution.py:9
  787.9 170.8 %all-reduce.27.cloned.1.call-start = ((), (), s32[]{:S(2)}) async-start(), calls=%async_computation.3 | async-start | bytes 327680 | tf_op jit(solution)/shard_map/psum | solution.py:55
  788.0 4.6 collective-permute-start.28
  901.4 215.3 %all-reduce.37.cloned.1.call-start = ((), (), s32[]{:S(2)}) async-start(), calls=%async_computation.8 | async-start | bytes 1310720 | tf_op jit(solution)/shard_map/psum | solution.py:9
  1037.3 170.5 %all-reduce.29.cloned.1.call-start = ((), (), s32[]{:S(2)}) async-start(), calls=%async_computation.4 | async-start | bytes 327680 | tf_op jit(solution)/shard_map/psum | solution.py:55
  1037.3 4.6 collective-permute-start.35
  1150.5 215.4 %all-reduce.35.cloned.1.call-start = ((), (), s32[]{:S(2)}) async-start(), calls=%async_computation.7 | async-start | bytes 1310720 | tf_op jit(solution)/shard_map/psum | solution.py:9
  1286.4 170.6 %all-reduce.31.cloned.1.call-start = ((), (), s32[]{:S(2)}) async-start(), calls=%async_computation.5 | async-start | bytes 327680 | tf_op jit(solution)/shard_map/psum | solution.py:55
  1399.7 213.7 %all-reduce.33.cloned.1.call-start = ((), (), s32[]{:S(2)}) async-start(), calls=%async_computation.6 | async-start | bytes 655360 | tf_op jit(solution)/shard_map/psum | solution.py:9
  (38 other events, 526.9 us)
Sparse Core Ops, SparseCore 0:
  41.7 83.5 all-reduce.44
  142.6 57.0 all-reduce.20
  278.4 79.3 all-reduce.42
  391.8 57.1 all-reduce.22
  527.6 79.3 all-reduce.40
  652.2 57.1 all-reduce.24
  788.1 79.3 all-reduce.38
  901.6 57.1 all-reduce.26
  1037.4 79.3 all-reduce.36
  1150.6 57.1 all-reduce.28
  1286.5 79.3 all-reduce.34
  1399.8 57.1 all-reduce.30
  1536.0 77.3 all-reduce.32
